TPU v7x, 512 devices: a whole 4x8x8 slice. The times are simulated.
512 devices in a mesh: dp: 32 (over y, x_lo, core), mp: 16 (over z, x_hi).
Axes of the slice: x: 4 (x_hi: 2, x_lo: 2; x = x_hi * 2 + x_lo), y: 8, z: 8, core: 2. Of those that a mesh axis runs over, the one named last changes fastest.
Arguments:
- hidden: bfloat16 [4096, 2048], P('dp', 'mp'), may hold values from -6 to 6
- q_weight: bfloat16 [2048, 3072], P('dp', 'mp'), may hold values from -0.125 to 0.125
- dkv_weight: bfloat16 [2048, 576], P('mp', 'dp'), may hold values from -0.125 to 0.125
- latent_gain: float32 [512], replicated, may hold values from 0.1 to 1.9
- kvb_weight: bfloat16 [512, 16, 256], P('dp', 'mp'), may hold values from -0.25 to 0.25
- out_weight: bfloat16 [2048, 2048], P('mp', 'dp'), may hold values from -0.125 to 0.125
- cache: bfloat16 [8192, 64, 576], P(('dp', 'mp')), may hold values from -200 to 200
- cache_len: int32 [64], P('dp'), may hold values from 64 to 8128
- draft_count: int32 [64], P('dp'), may hold values from 32 to 64
- parents: int32 [64, 64], P('dp'), may hold values from 0 to 62, as said below
- accept_node: int32 [64], P('dp'), may hold values from 0 to 63, as said below
- page_table: int32 [64, 128], P('dp'), may hold values from 0 to 255, as said below
Outputs:
- attended: bfloat16 [4096, 2048], P(('dp', 'mp'))
- new_cache: bfloat16 [8192, 64, 576], P(('dp', 'mp'))
Inputs may be any that keep to these rules, and one draw needn't show every extreme that they name: `page_table`: within each group of 2 consecutive requests the entries are a permutation of 0 to 255; entry v is slot v % 16 of the group's device v // 16 along mp. parents[q, 0] = 0 and parents[q, i] < i for i >= 1. `accept_node`: less than the request's draft_count.
All inputs are finite; a program needn't handle non-finite values.
Results may differ from a plain program's by a relative error of at most 0.03.
Values may be sent and summed in bfloat16 or wider, within the bound.
No kernel may reach another device: no remote copies, remote signals or barrier semaphores. Data moves between devices by JAX's collectives and lax.ppermute only.
A program may use at most 64 MiB of HBM per device.

v0:
```python
import jax
import jax.numpy as jnp
from jax import lax
from jax.sharding import PartitionSpec as P

NOPE = 128
ROPE = 64
LAT = 512


def tree_reach(parent_row):
    count = parent_row.shape[0]
    index = jnp.arange(count, dtype=jnp.int32)
    linked = jnp.logical_or(
        parent_row[:, None] == index[None, :], index[:, None] == index[None, :]
    ).astype(jnp.float32)
    for _ in range(max(1, (count - 1).bit_length())):
        linked = jnp.minimum(jnp.dot(linked, linked, precision=lax.Precision.HIGHEST), 1.0)
    return linked


def angles(positions, width):
    half_dim = width // 2
    inverse = 10000.0 ** (-(jnp.arange(half_dim, dtype=jnp.float32) * 2.0) / width)
    phase = positions[..., None] * inverse
    return (jnp.cos(phase), jnp.sin(phase))


def rotary(values, cosine, sine):
    half_dim = values.shape[-1] // 2
    first = values[..., :half_dim]
    second = values[..., half_dim:]
    return jnp.concatenate(
        [first * cosine - second * sine, second * cosine + first * sine], axis=-1
    )


def lookup(index_rows, table):
    choices_hot = index_rows[:, None] == jnp.arange(table.shape[0], dtype=jnp.int32)[None, :]
    return jnp.sum(jnp.where(choices_hot, table[None, :], jnp.zeros((), table.dtype)), axis=1)


def tree_part(q_rows, fresh_req, linked, value_maps, scale_val):
    reqs, draft, heads, width = q_rows.shape
    tree_scores = (
        jnp.einsum("rthc,rjc->rthj", q_rows, fresh_req, preferred_element_type=jnp.float32)
        * scale_val
    )
    tree_live = (linked > 0.5)[:, :, None, :]
    tree_top = jnp.max(jnp.where(tree_live, tree_scores, -1e30), axis=3)
    tree_weights = jnp.where(tree_live, jnp.exp(tree_scores - tree_top[..., None]), 0.0)
    tree_sum = jnp.sum(tree_weights, axis=3).reshape(reqs * draft, heads)
    tree_lat = jnp.einsum(
        "rthj,rjl->rthl",
        tree_weights.astype(jnp.bfloat16),
        fresh_req[..., :LAT],
        preferred_element_type=jnp.float32,
    )
    tree_v = jnp.einsum(
        "thl,lhv->thv",
        tree_lat.reshape(reqs * draft, heads, LAT),
        value_maps.astype(jnp.float32),
        precision=lax.Precision.HIGHEST,
    )
    return (tree_top.reshape(reqs * draft, heads), tree_sum, tree_v)


def joined(cache_top, cache_v, cache_sum, tree_top, tree_sum, tree_v):
    joint = jnp.maximum(cache_top, tree_top)
    left_scale = jnp.exp(cache_top - joint)
    right_scale = jnp.exp(tree_top - joint)
    combined = (cache_v * left_scale[..., None] + tree_v * right_scale[..., None]) / (
        cache_sum * left_scale + tree_sum * right_scale
    )[..., None]
    return combined.astype(jnp.bfloat16).reshape(
        combined.shape[0], combined.shape[1] * combined.shape[2]
    )


def per_device(
    hidden,
    q_weight,
    dkv_weight,
    latent_gain,
    kvb_weight,
    out_weight,
    cache,
    cache_len,
    draft_count,
    parents,
    accept_node,
    page_table,
):
    highest = lax.Precision.HIGHEST
    mp_size = lax.axis_size("mp")
    mp_rank = lax.axis_index("mp")
    reqs, draft = parents.shape
    tokens = reqs * draft
    heads_mine = kvb_weight.shape[1]
    heads_all = heads_mine * mp_size
    slot_count, page_len, width = cache.shape
    scale_val = (NOPE + ROPE) ** (-0.5)
    share = tokens // mp_size
    full_x = lax.all_gather(hidden, "mp", axis=1, tiled=True)
    query = jnp.dot(
        full_x,
        lax.all_gather(q_weight, "dp", axis=0, tiled=True),
        preferred_element_type=jnp.float32,
    )
    query = query.astype(jnp.bfloat16).reshape(tokens, heads_mine, NOPE + ROPE)
    linked = jax.vmap(tree_reach)(parents)
    depth = jnp.sum(linked, axis=2) - 1.0
    positions = (cache_len.astype(jnp.float32)[:, None] + depth).reshape(tokens)
    cosine, sine = angles(positions, ROPE)
    down_cols = lax.all_gather(dkv_weight, "dp", axis=1, tiled=True)
    down_full = lax.all_gather(down_cols, "mp", axis=0, tiled=True)
    compressed = jnp.dot(full_x, down_full, preferred_element_type=jnp.float32)
    latent = compressed[:, :LAT]
    normed = (
        latent * lax.rsqrt(jnp.mean(latent * latent, axis=-1, keepdims=True) + 1e-06) * latent_gain
    )
    fresh = jnp.concatenate([normed, rotary(compressed[:, LAT:], cosine, sine)], axis=-1).astype(
        jnp.bfloat16
    )
    fresh_req = fresh.reshape(reqs, draft, width)
    up_maps = lax.all_gather(kvb_weight, "dp", axis=0, tiled=True)
    q_rope = rotary(query[..., NOPE:].astype(jnp.float32), cosine[:, None, :], sine[:, None, :])
    q_latent = jnp.einsum(
        "thn,lhn->thl", query[..., :NOPE], up_maps[:, :, :NOPE], preferred_element_type=jnp.float32
    )
    mine_abs = jnp.concatenate([q_latent, q_rope], axis=-1).astype(jnp.bfloat16)
    q_all = lax.all_gather(mine_abs, "mp", axis=1, tiled=True)
    value_all = lax.all_gather(up_maps[:, :, NOPE:], "mp", axis=1, tiled=True)
    slot_ids = mp_rank * slot_count + jnp.arange(slot_count, dtype=jnp.int32)
    matched = (page_table[:, :, None] == slot_ids[None, None, :]).astype(jnp.int32)
    slot_req = jnp.sum(matched * jnp.arange(reqs, dtype=jnp.int32)[:, None, None], axis=(0, 1))
    slot_page = jnp.sum(
        matched * jnp.arange(page_table.shape[1], dtype=jnp.int32)[None, :, None], axis=(0, 1)
    )
    key_pos = (
        slot_page[:, None] * page_len + jnp.arange(page_len, dtype=jnp.int32)[None, :]
    ).reshape(slot_count * page_len)
    key_req = jnp.repeat(slot_req, page_len)
    keys = cache.reshape(slot_count * page_len, width)
    top_list = []
    sum_list = []
    out_list = []
    for request in range(reqs):
        rows = q_all[request * draft : (request + 1) * draft].reshape(draft * heads_all, width)
        scores = (
            lax.dot_general(
                rows, keys, (((1,), (1,)), ((), ())), preferred_element_type=jnp.float32
            )
            * scale_val
        )
        live = jnp.logical_and(key_req == request, key_pos < cache_len[request])[None, :]
        top_row = jnp.max(jnp.where(live, scores, -1e30), axis=1)
        weights = jnp.where(live, jnp.exp(scores - top_row[:, None]), 0.0)
        top_list.append(top_row)
        sum_list.append(jnp.sum(weights, axis=1))
        out_list.append(
            jnp.dot(weights.astype(jnp.bfloat16), keys[:, :LAT], preferred_element_type=jnp.float32)
        )
    local_top = jnp.concatenate(top_list).reshape(tokens, heads_all)
    local_sum = jnp.concatenate(sum_list).reshape(tokens, heads_all)
    local_out = jnp.concatenate(out_list, axis=0).reshape(tokens, heads_all, LAT)
    global_top = lax.pmax(local_top, "mp")
    factor = jnp.exp(local_top - global_top)
    partial_v = jnp.einsum(
        "thl,lhv->thv",
        local_out * factor[..., None],
        value_all.astype(jnp.float32),
        precision=highest,
    )
    out_full = lax.all_gather(out_weight, "dp", axis=1, tiled=True)
    row_index = mp_rank * share + jnp.arange(share, dtype=jnp.int32)
    cache_v, cache_sum = (
        lax.psum_scatter(
            partial_v.astype(jnp.bfloat16), "mp", scatter_dimension=1, tiled=True
        ).astype(jnp.float32),
        lax.psum_scatter(
            (local_sum * factor).astype(jnp.bfloat16), "mp", scatter_dimension=1, tiled=True
        ).astype(jnp.float32),
    )
    mine_top = lax.dynamic_slice_in_dim(global_top, mp_rank * heads_mine, heads_mine, 1)
    mine_q = lax.dynamic_slice_in_dim(q_all, mp_rank * heads_mine, heads_mine, 1)
    tree_top, tree_sum, tree_v = tree_part(
        mine_q.reshape(reqs, draft, heads_mine, width),
        fresh_req,
        linked,
        up_maps[:, :, NOPE:],
        scale_val,
    )
    head_out = joined(mine_top, cache_v, cache_sum, tree_top, tree_sum, tree_v)
    mine_rows = lax.psum_scatter(
        jnp.dot(head_out, out_full, preferred_element_type=jnp.float32).astype(jnp.bfloat16),
        "mp",
        scatter_dimension=0,
        tiled=True,
    ).astype(jnp.float32)
    row_count = lookup(row_index // draft, draft_count)
    attended = jnp.where((row_index % draft < row_count)[:, None], mine_rows, 0.0).astype(
        jnp.bfloat16
    )
    accept_hot = (accept_node[:, None] == jnp.arange(draft, dtype=jnp.int32)[None, :]).astype(
        jnp.float32
    )
    path = jnp.einsum("ri,rij->rj", accept_hot, linked, precision=highest)
    deepest = jnp.sum(path, axis=1) - 1.0
    picker = jnp.logical_and(
        path[:, None, :] > 0.5,
        depth[:, None, :] == jnp.arange(draft, dtype=jnp.int32).astype(jnp.float32)[None, :, None],
    )
    entries = jnp.einsum(
        "rdt,rtc->rdc", picker.astype(jnp.bfloat16), fresh_req, preferred_element_type=jnp.float32
    )
    entries = entries.astype(jnp.bfloat16).reshape(tokens, width)
    key_len = lookup(key_req, cache_len)
    key_deep = lookup(key_req, deepest)
    offset = key_pos - key_len
    column = jnp.arange(tokens, dtype=jnp.int32)
    chosen = jnp.logical_and(
        key_req[:, None] == (column // draft)[None, :], offset[:, None] == (column % draft)[None, :]
    )
    chosen = jnp.logical_and(chosen, (offset.astype(jnp.float32) <= key_deep)[:, None])
    placed = jnp.dot(
        chosen.astype(jnp.bfloat16), entries, preferred_element_type=jnp.float32
    ).astype(jnp.bfloat16)
    new_cache = jnp.where(jnp.any(chosen, axis=1)[:, None], placed, keys).reshape(cache.shape)
    return (attended, new_cache)


def solution(mesh):
    return jax.shard_map(
        per_device,
        mesh=mesh,
        in_specs=(
            P("dp", "mp"),
            P("dp", "mp"),
            P("mp", "dp"),
            P(),
            P("dp", "mp", None),
            P("mp", "dp"),
            P(("dp", "mp"), None, None),
            P("dp"),
            P("dp"),
            P("dp", None),
            P("dp"),
            P("dp", None),
        ),
        out_specs=(P(("dp", "mp"), None), P(("dp", "mp"), None, None)),
        check_vma=False,
    )
```

profile of v0, /device:TPU:8, one launch (start us, length us, event | category | flops | bytes accessed | tf_op | source)
XLA Modules:
  0.0 832.7 jit_solution(14350531714993052761)
XLA Ops:
  7.3 1.0 convolution_minimum_fusion.5
  8.3 0.2 convolution_minimum_fusion.4
  8.5 0.2 convolution_minimum_fusion.3
  8.7 0.2 convolution_minimum_fusion.2
  8.9 0.2 convolution_minimum_fusion.1
  9.1 0.3 fusion.97
  9.4 0.7 convert_element_type.86
  10.2 50.1 %all_gather.24 = bf16[128,2048]{1,0:T(8,128)(2,1)S(1)} all-gather(bf16[128,128]{1,0:T(8,128)(2,1)} %param.12), channel_id=1, replica_groups=mesh['dp'=32,'mp'=16] {'mp'}, dimensions={1}, use_global_device_ids=true | all-gather | bytes 557056 | tf_op jit(solution)/shard_map/all_gather | solution.py:104
  60.3 34.8 %all_gather.25 = bf16[2048,192]{1,0:T(8,128)(2,1)S(1)} all-gather(bf16[64,192]{1,0:T(8,128)(2,1)} %param.13), channel_id=1, replica_groups=mesh['dp'=32,'mp'=16] {'dp'}, dimensions={0}, use_global_device_ids=true | all-gather | bytes 811008 | tf_op jit(solution)/shard_map/all_gather | solution.py:107
  95.1 0.5 fusion.26
  95.6 0.1 fusion.72
  95.8 0.1 copy.81
  95.9 0.1 copy.82
  96.1 31.4 %all_gather.26 = bf16[512,1,256]{2,0,1:T(8,128)(2,1)S(1)} all-gather(bf16[16,1,256]{2,0,1:T(8,128)(2,1)S(1)} %copy-done.8), channel_id=1, replica_groups=mesh['dp'=32,'mp'=16] {'dp'}, dimensions={0}, use_global_device_ids=true | all-gather | bytes 270336 | tf_op jit(solution)/shard_map/all_gather | solution.py:126
  127.5 0.2 fusion.21
  127.7 0.1 pad_maximum_fusion.1
  127.8 0.8 copy.83
  128.6 32.6 %all-gather = bf16[32,18,128]{2,1,0:T(8,128)(2,1)S(1)} all-gather(bf16[1,18,128]{2,1,0:T(8,128)(2,1)S(1)} %bitcast.116), channel_id=1, replica_groups=mesh['dp'=32,'mp'=16] {'dp'}, dimensions={0}, use_global_device_ids=true | all-gather | bytes 152064 | tf_op jit(solution)/shard_map/all_gather | solution.py:115
  161.2 0.7 reshape.428
  162.0 0.7 slice.70
  162.7 0.7 fusion.96
  163.4 0.2 fusion.65
  163.8 0.1 fusion.78
  164.0 0.1 reduce_sum.108
  164.4 32.7 %all_gather.31 = bf16[128,2048]{0,1:T(8,128)(2,1)S(1)} all-gather(bf16[128,64]{0,1:T(8,128)(2,1)S(1)} %copy-done.7), channel_id=1, replica_groups=mesh['dp'=32,'mp'=16] {'dp'}, dimensions={1}, use_global_device_ids=true | all-gather | bytes 540672 | tf_op jit(solution)/shard_map/all_gather | solution.py:175
  197.2 1.5 copy.98
  198.7 1.2 dynamic-slice
  200.0 1.3 convert_compare_fusion
  201.3 1.0 fusion.31
  202.4 16.0 %all-gather.5.cloned.1.call-done = bf16[128,16,576]{0,2,1:T(8,128)(2,1)} async-done(((bf16[128,1,576]{0,2,1:T(8,128)(2,1)}), bf16[128,16,576]{0,2,1:T(8,128)(2,1)}) %all-gather.5.cloned.1.call-update) | async-done | bytes 2359312 | tf_op jit(solution)/shard_map/all_gather | solution.py:132
  218.4 4.7 fusion.95
  223.1 4.5 copy.85
  227.6 3.4 copy.84
  231.0 5.6 select_reduce_fusion.1
  236.7 5.2 select_reduce_fusion
  241.9 4.5 fusion.1
  247.0 39.1 %pmax.7 = f32[128,16]{0,1:T(8,128)S(1)} all-reduce(f32[128,16]{0,1:T(8,128)S(1)} %pad_maximum_fusion.5), channel_id=1, replica_groups=mesh['dp'=32,'mp'=16] {'mp'}, use_global_device_ids=true, to_apply=%region_6.7 | all-reduce | flops 2048 | bytes 16384 | tf_op jit(solution)/shard_map/pmax | solution.py:167
  286.1 0.1 copy.96
  286.2 73.8 %all-reduce = bf16[128,16]{1,0:T(8,128)(2,1)S(1)} all-reduce(bf16[128,16]{1,0:T(8,128)(2,1)S(1)} %copy.96), channel_id=3, replica_groups=mesh['dp'=32,'mp'=16] {'mp'}, use_global_device_ids=true, to_apply=%region_12.13.clone | all-reduce | flops 2048 | bytes 8192
  360.1 2.4 fusion.98
  362.6 0.1 fusion.68
  362.8 3.8 fusion.7
  366.6 1.5 fusion.5
  368.0 2.4 pad_maximum_fusion
  370.4 33.0 %all-gather.7.cloned.1.call-done = bf16[512,16,128]{2,0,1:T(8,128)(2,1)} async-done(((bf16[512,1,128]{2,0,1:T(8,128)(2,1)}), bf16[512,16,128]{2,0,1:T(8,128)(2,1)}) %all-gather.7.cloned.1.call-update) | async-done | bytes 2097168 | tf_op jit(solution)/shard_map/all_gather | solution.py:133
  403.4 7.9 fusion.20
  411.4 1.0 constant_dynamic-slice_fusion.1
  412.4 0.6 constant_dynamic-slice_fusion
  413.1 0.2 copy.89
  413.3 0.1 copy.105
  413.4 0.1 copy.106
  413.5 0.1 multiply_convert_fusion
  413.7 0.1 copy.90
  413.8 0.3 fusion.40
  414.2 0.2 fusion.45
  414.5 0.2 fusion.47
  414.8 200.4 %reduce-scatter.4.cloned.1.call-done = bf16[128,1,128]{2,0,1:T(8,128)(2,1)} async-done(((bf16[128,16,128]{2,0,1:T(8,128)(2,1)}), bf16[128,1,128]{2,0,1:T(8,128)(2,1)}) %reduce-scatter.4.cloned.1.call-update) | async-done | bytes 32784 | tf_op jit(solution)/shard_map/reduce_scatter | solution.py:178
  615.1 1.0 fusion.28
  616.1 1.1 convolution_convert_fusion
  617.3 0.2 convolution_convert_fusion.2
  617.6 1.6 fusion.18
  619.2 1.4 copy.99
  620.6 204.1 %reduce-scatter.6.cloned.1.call-done = bf16[8,2048]{1,0:T(8,128)(2,1)} async-done(((bf16[128,2048]{1,0:T(8,128)(2,1)}), bf16[8,2048]{1,0:T(8,128)(2,1)}) %reduce-scatter.6.cloned.1.call-update) | async-done | bytes 32784 | tf_op jit(solution)/shard_map/reduce_scatter | solution.py:195
  824.7 1.4 select_convert_fusion
  (79 shorter events, 2.3 us)
Async XLA Ops:
  7.2 155.6 %copy-start.10 = (s32[2]{0:T(128)S(1)}, s32[2]{0:T(128)}, u32[]{:S(2)}) copy-start(s32[2]{0:T(128)} %param.19) | copy-start | bytes 28
  7.2 88.9 %copy-start.8 = (bf16[16,1,256]{2,0,1:T(8,128)(2,1)S(1)}, bf16[16,1,256]{2,0,1:T(8,128)(2,1)}, u32[]{:S(2)}) copy-start(bf16[16,1,256]{2,0,1:T(8,128)(2,1)} %param.16) | copy-start | bytes 24580
  7.2 121.4 %copy-start.9 = (bf16[128,18]{0,1:T(8,128)(2,1)S(1)}, bf16[128,18]{0,1:T(8,128)(2,1)}, u32[]{:S(2)}) copy-start(bf16[128,18]{0,1:T(8,128)(2,1)} %param.14) | copy-start | bytes 13828
  7.2 156.2 %copy-start.12 = (s32[2,128]{1,0:T(2,128)S(1)}, s32[2,128]{1,0:T(2,128)}, u32[]{:S(2)}) copy-start(s32[2,128]{1,0:T(2,128)} %param.23) | copy-start | bytes 3076
  7.2 156.5 %copy-start.13 = (s32[2]{0:T(128)S(1)}, s32[2]{0:T(128)}, u32[]{:S(2)}) copy-start(s32[2]{0:T(128)} %param.22) | copy-start | bytes 28
  7.2 157.2 %copy-start.7 = (bf16[128,64]{0,1:T(8,128)(2,1)S(1)}, bf16[128,64]{0,1:T(8,128)(2,1)}, u32[]{:S(2)}) copy-start(bf16[128,64]{0,1:T(8,128)(2,1)} %param.17) | copy-start | bytes 49156
  7.2 190.0 %copy-start.2 = (bf16[16,64,576]{2,1,0:T(8,128)(2,1)S(1)}, bf16[16,64,576]{2,1,0:T(8,128)(2,1)}, u32[]{:S(2)}) copy-start(bf16[16,64,576]{2,1,0:T(8,128)(2,1)} %param.18) | copy-start | bytes 3538948
  7.2 211.2 %all-gather.5.cloned.1.call-start = ((), (), s32[]{:S(2)}) async-start(), calls=%async_computation.2 | async-start | bytes 2506752 | tf_op jit(solution)/shard_map/all_gather | solution.py:132
  60.3 139.6 %copy-start.14 = (s32[2]{0:T(128)S(1)}, s32[2]{0:T(128)}, u32[]{:S(2)}) copy-start(s32[2]{0:T(128)} %param.20) | copy-start | bytes 28
  127.5 74.9 %copy-start.5 = (bf16[512,1,256]{2,0,1:T(8,128)(2,1)}, bf16[512,1,256]{2,0,1:T(8,128)(2,1)S(1)}, u32[]{:S(2)}) copy-start(bf16[512,1,256]{2,0,1:T(8,128)(2,1)S(1)} %all_gather.26) | copy-start | bytes 786436
  128.6 231.5 %all-gather.9.cloned.1.call-start = ((), (), s32[]{:S(2)}) async-start(), calls=%async_computation.5 | async-start | bytes 2506752 | tf_op jit(solution)/shard_map/all_gather | solution.py:116
  161.9 241.5 %all-gather.7.cloned.1.call-start = ((), (), s32[]{:S(2)}) async-start(), calls=%async_computation.3 | async-start | bytes 2228224 | tf_op jit(solution)/shard_map/all_gather | solution.py:133
  162.7 452.4 %reduce-scatter.4.cloned.1.call-start = ((), (), s32[]{:S(2)}) async-start(), calls=%async_computation.4 | async-start | bytes 557056 | tf_op jit(solution)/shard_map/reduce_scatter | solution.py:178
  231.0 5.7 copy-start.1
  241.9 120.8 %copy-start.3 = (bf16[16,64,576]{2,1,0:T(8,128)(2,1)S(1)}, bf16[16,64,576]{2,1,0:T(8,128)(2,1)}, u32[]{:S(2)}) copy-start(bf16[16,64,576]{2,1,0:T(8,128)(2,1)} %param.18) | copy-start | bytes 3538948
  362.8 3.8 copy-start
  370.4 43.1 %copy-start.11 = (f32[512]{0:T(512)S(1)}, f32[512]{0:T(512)}, u32[]{:S(2)}) copy-start(f32[512]{0:T(512)} %param.15) | copy-start | bytes 6148
  403.4 211.7 %copy-start.6 = (bf16[512,1,256]{2,0,1:T(8,128)(2,1)S(1)}, bf16[512,1,256]{2,0,1:T(8,128)(2,1)}, u32[]{:S(2)}) copy-start(bf16[512,1,256]{2,0,1:T(8,128)(2,1)} %copy-done.5) | copy-start | bytes 786436
  411.3 206.2 %copy-start.4 = (bf16[1024,576]{0,1:T(8,128)(2,1)S(1)}, bf16[1024,576]{0,1:T(8,128)(2,1)}, u32[]{:S(2)}) copy-start(bf16[1024,576]{0,1:T(8,128)(2,1)} %copy.98) | copy-start | bytes 3538948
  411.3 413.4 %reduce-scatter.6.cloned.1.call-start = ((), (), s32[]{:S(2)}) async-start(), calls=%async_computation.6 | async-start | bytes 557056 | tf_op jit(solution)/shard_map/reduce_scatter | solution.py:195
Sparse Core Ops, SparseCore 0:
  128.7 89.6 all-gather.4
  221.4 90.6 all-gather.8
  315.3 88.0 all-gather.6
  411.5 203.6 reduce-scatter.3
  620.0 204.7 reduce-scatter.5
where the time goes:
time: 833 us
  waiting for transfers between devices  454 us (55%)
  blocking collectives  294 us (35%)
  matrix products  33.8 us (4%)
  local copies, waits for them, and re-layouts  23.3 us (3%)
  between operations  14.2 us (2%)
  other arithmetic  13.2 us (2%)
    reduce_scatter x1, waiting for transfers between devices, per_device(): lax.psum_scatter(jnp.dot(head_out, out_full, preferred_element_type=jnp.f...  204 us
    reduce_scatter x1, waiting for transfers between devices, per_device(): lax.psum_scatter(partial_v.astype(jnp.bfloat16), 'mp', scatter_dimension=...  200 us
    unnamed x1, blocking collectives  73.8 us
    all_gather x1, blocking collectives, per_device(): full_x = lax.all_gather(hidden, 'mp', axis=1, tiled=True)  50.1 us
    pmax x1, blocking collectives, per_device(): global_top = lax.pmax(local_top, 'mp')  39.1 us
    all_gather x1, blocking collectives, per_device(): lax.all_gather(q_weight, 'dp', axis=0, tiled=True)  34.8 us
    all_gather x1, waiting for transfers between devices, per_device(): value_all = lax.all_gather(up_maps[:, :, NOPE:], 'mp', axis=1, tiled=True)  33 us
    all_gather x1, blocking collectives, per_device(): out_full = lax.all_gather(out_weight, 'dp', axis=1, tiled=True)  32.7 us
  transfers between devices with their start and end apart: 5, of which 4 were waited for; matrix products, arithmetic and copies ran while one was open for 6% of the time, Pallas kernels for 0%

commit v1 on v0

--- a/solution.py
+++ b/solution.py
@@ -104,7 +104,9 @@
     full_x = lax.all_gather(hidden, "mp", axis=1, tiled=True)
     query = jnp.dot(
         full_x,
-        lax.all_gather(q_weight, "dp", axis=0, tiled=True),
+        jnp.concatenate(
+            lax.all_to_all(jnp.stack([q_weight] * lax.axis_size("dp")), "dp", 0, 0), axis=0
+        ),
         preferred_element_type=jnp.float32,
     )
     query = query.astype(jnp.bfloat16).reshape(tokens, heads_mine, NOPE + ROPE)

time: 833 us -> 765 us (0.918)
  waiting for transfers between devices: 454 us -> 394 us
  blocking collectives: 294 us -> 276 us
    reduce_scatter x1, waiting for transfers between devices: 200 us -> 127 us  [per_device(): lax.psum_scatter(partial_v.astype(jnp.bfloat16), 'mp', scatter_dimension=...]
    all_gather x1 -> x0, blocking collectives: 34.8 us -> none  [per_device(): lax.all_gather(q_weight, 'dp', axis=0, tiled=True)]
    all_gather x1, waiting for transfers between devices: 16 us -> 46.8 us  [per_device(): q_all = lax.all_gather(mine_abs, 'mp', axis=1, tiled=True)]
    all_gather x1, waiting for transfers between devices: 33 us -> 16.1 us  [per_device(): value_all = lax.all_gather(up_maps[:, :, NOPE:], 'mp', axis=1, tiled=True)]
    all_gather x1, blocking collectives: 31.4 us -> 46.2 us  [per_device(): up_maps = lax.all_gather(kvb_weight, 'dp', axis=0, tiled=True)]
  transfers between devices with their start and end apart: 5 -> 6, of which waited for: 4 -> 4; matrix products, arithmetic and copies ran while one was open for 6% -> 8% of each run, Pallas kernels for 0% -> 0%
where the time goes in v1:
time: 765 us; the launch traced here: 764 us
  waiting for transfers between devices  394 us (52%)
  blocking collectives  276 us (36%)
  matrix products  33.7 us (4%)
  local copies, waits for them, and re-layouts  26.1 us (3%)
  between operations  14.1 us (2%)
  other arithmetic  13.8 us (2%)
    reduce_scatter x1, waiting for transfers between devices, per_device(): lax.psum_scatter(jnp.dot(head_out, out_full, preferred_element_type=jnp.f...  204 us
    reduce_scatter x1, waiting for transfers between devices, per_device(): lax.psum_scatter(partial_v.astype(jnp.bfloat16), 'mp', scatter_dimension=...  127 us
    unnamed x1, blocking collectives  73.2 us
    all_gather x1, blocking collectives, per_device(): full_x = lax.all_gather(hidden, 'mp', axis=1, tiled=True)  50.6 us
    all_gather x1, waiting for transfers between devices, per_device(): q_all = lax.all_gather(mine_abs, 'mp', axis=1, tiled=True)  46.8 us
    all_gather x1, blocking collectives, per_device(): up_maps = lax.all_gather(kvb_weight, 'dp', axis=0, tiled=True)  46.2 us
    pmax x1, blocking collectives, per_device(): global_top = lax.pmax(local_top, 'mp')  39.1 us
    all_gather x1, blocking collectives, per_device(): down_cols = lax.all_gather(dkv_weight, 'dp', axis=1, tiled=True)  34.4 us
  transfers between devices with their start and end apart: 6, of which 4 were waited for; matrix products, arithmetic and copies ran while one was open for 8% of the time, Pallas kernels for 0%

profile of v1, /device:TPU:8, one launch (start us, length us, event | category | flops | bytes accessed | tf_op | source)
XLA Modules:
  0.0 764.1 jit_solution(12952726337259196874)
XLA Ops:
  7.2 34.4 %all-gather = bf16[32,18,128]{2,1,0:T(8,128)(2,1)S(1)} all-gather(bf16[1,18,128]{2,1,0:T(8,128)(2,1)} %bitcast.118), channel_id=1, replica_groups=mesh['dp'=32,'mp'=16] {'dp'}, dimensions={0}, use_global_device_ids=true | all-gather | bytes 152064 | tf_op jit(solution)/shard_map/all_gather | solution.py:117
  41.6 0.7 reshape.434
  42.4 1.9 stack.2
  44.2 6.3 all-to-all-start
  50.6 0.7 convert_element_type.86
  51.3 1.0 convolution_minimum_fusion.5
  52.2 0.2 convolution_minimum_fusion.4
  52.4 0.2 convolution_minimum_fusion.3
  52.6 0.2 convolution_minimum_fusion.2
  52.8 0.2 convolution_minimum_fusion.1
  53.0 0.3 fusion.97
  53.5 46.2 %all_gather.22 = bf16[512,1,256]{2,0,1:T(8,128)(2,1)S(1)} all-gather(bf16[16,1,256]{2,0,1:T(8,128)(2,1)S(1)} %copy-done.7), channel_id=1, replica_groups=mesh['dp'=32,'mp'=16] {'dp'}, dimensions={0}, use_global_device_ids=true | all-gather | bytes 270336 | tf_op jit(solution)/shard_map/all_gather | solution.py:128
  99.7 50.6 %all_gather.21 = bf16[128,2048]{1,0:T(8,128)(2,1)S(1)} all-gather(bf16[128,128]{1,0:T(8,128)(2,1)S(1)} %copy-done.5), channel_id=1, replica_groups=mesh['dp'=32,'mp'=16] {'mp'}, dimensions={1}, use_global_device_ids=true | all-gather | bytes 557056 | tf_op jit(solution)/shard_map/all_gather | solution.py:104
  150.3 0.5 fusion.26
  150.8 0.1 fusion.72
  151.0 0.1 copy.81
  151.1 0.1 copy.82
  151.2 0.2 fusion.21
  151.5 0.8 copy.83
  152.4 0.7 slice.70
  153.1 0.6 fusion.96
  153.8 0.2 fusion.65
  154.2 0.1 fusion.78
  154.3 0.1 reduce_sum.108
  154.8 32.2 %all_gather.27 = bf16[128,2048]{0,1:T(8,128)(2,1)S(1)} all-gather(bf16[128,64]{0,1:T(8,128)(2,1)S(1)} %copy-done.6), channel_id=1, replica_groups=mesh['dp'=32,'mp'=16] {'dp'}, dimensions={1}, use_global_device_ids=true | all-gather | bytes 540672 | tf_op jit(solution)/shard_map/all_gather | solution.py:177
  187.0 2.4 copy.98
  189.5 1.3 dynamic-slice
  190.8 1.3 convert_compare_fusion
  192.1 1.0 fusion.31
  193.2 2.4 fusion.98
  195.7 0.8 multiply_convert_fusion
  196.5 46.8 %all-gather.5.cloned.1.call-done = bf16[128,16,576]{0,2,1:T(8,128)(2,1)} async-done(((bf16[128,1,576]{0,2,1:T(8,128)(2,1)}), bf16[128,16,576]{0,2,1:T(8,128)(2,1)}) %all-gather.5.cloned.1.call-update) | async-done | bytes 2359312 | tf_op jit(solution)/shard_map/all_gather | solution.py:134
  243.3 4.7 fusion.95
  248.0 4.5 copy.85
  252.5 3.4 copy.84
  255.9 5.6 select_reduce_fusion.1
  261.6 5.1 select_reduce_fusion
  266.9 4.5 fusion.1
  271.8 0.1 pad_maximum_fusion.5
  271.9 39.1 %pmax.7 = f32[128,16]{0,1:T(8,128)S(1)} all-reduce(f32[128,16]{0,1:T(8,128)S(1)} %pad_maximum_fusion.5), channel_id=1, replica_groups=mesh['dp'=32,'mp'=16] {'mp'}, use_global_device_ids=true, to_apply=%region_6.7 | all-reduce | flops 2048 | bytes 16384 | tf_op jit(solution)/shard_map/pmax | solution.py:169
  311.1 3.8 fusion.7
  314.9 1.5 fusion.5
  316.4 2.4 pad_maximum_fusion
  318.7 16.1 %all-gather.7.cloned.1.call-done = bf16[512,16,128]{2,0,1:T(8,128)(2,1)} async-done(((bf16[512,1,128]{2,0,1:T(8,128)(2,1)}), bf16[512,16,128]{2,0,1:T(8,128)(2,1)}) %all-gather.7.cloned.1.call-update) | async-done | bytes 2097168 | tf_op jit(solution)/shard_map/all_gather | solution.py:135
  334.8 7.8 %fusion.20 = bf16[128,16,128]{2,0,1:T(8,128)(2,1)} fusion(bf16[512,16,128]{2,0,1:T(8,128)(2,1)} %all-gather.7.cloned.1.call-done, f32[128,16,512]{2,1,0:T(8,128)} %bitcast.98, f32[128,16]{0,1:T(8,128)S(1)} %get-tuple-element.12), kind=kOutput, calls=%fused_computation.26 | convolution fusion | flops 1611923456 | bytes 6823936 | tf_op jit(solution)/shard_map/thl,lhv->thv/dot_general | solution.py:171
  342.7 0.1 fusion.68
  342.9 0.1 copy.105
  343.0 0.1 copy.106
  343.3 0.1 copy.96
  343.4 73.2 %all-reduce = bf16[128,16]{1,0:T(8,128)(2,1)S(1)} all-reduce(bf16[128,16]{1,0:T(8,128)(2,1)S(1)} %copy.96), channel_id=3, replica_groups=mesh['dp'=32,'mp'=16] {'mp'}, use_global_device_ids=true, to_apply=%region_12.13.clone | all-reduce | flops 2048 | bytes 8192
  416.6 0.7 constant_dynamic-slice_fusion
  417.3 0.9 constant_dynamic-slice_fusion.1
  418.3 0.2 copy.89
  418.5 0.3 fusion.40
  418.9 0.2 fusion.45
  419.2 0.2 fusion.47
  419.4 127.0 %reduce-scatter.4.cloned.1.call-done = bf16[128,1,128]{2,0,1:T(8,128)(2,1)} async-done(((bf16[128,16,128]{2,0,1:T(8,128)(2,1)}), bf16[128,1,128]{2,0,1:T(8,128)(2,1)}) %reduce-scatter.4.cloned.1.call-update) | async-done | bytes 32784 | tf_op jit(solution)/shard_map/reduce_scatter | solution.py:180
  546.4 1.0 fusion.28
  547.4 1.1 convolution_convert_fusion
  548.6 0.2 convolution_convert_fusion.2
  548.8 1.6 fusion.18
  550.4 1.4 copy.99
  551.9 204.2 %reduce-scatter.6.cloned.1.call-done = bf16[8,2048]{1,0:T(8,128)(2,1)} async-done(((bf16[128,2048]{1,0:T(8,128)(2,1)}), bf16[8,2048]{1,0:T(8,128)(2,1)}) %reduce-scatter.6.cloned.1.call-update) | async-done | bytes 32784 | tf_op jit(solution)/shard_map/reduce_scatter | solution.py:197
  756.1 1.4 select_convert_fusion
  (77 shorter events, 2.4 us)
Async XLA Ops:
  7.2 46.3 %copy-start.7 = (bf16[16,1,256]{2,0,1:T(8,128)(2,1)S(1)}, bf16[16,1,256]{2,0,1:T(8,128)(2,1)}, u32[]{:S(2)}) copy-start(bf16[16,1,256]{2,0,1:T(8,128)(2,1)} %param.16) | copy-start | bytes 24580
  7.2 92.5 %copy-start.5 = (bf16[128,128]{1,0:T(8,128)(2,1)S(1)}, bf16[128,128]{1,0:T(8,128)(2,1)}, u32[]{:S(2)}) copy-start(bf16[128,128]{1,0:T(8,128)(2,1)} %param.12) | copy-start | bytes 98308
  7.2 186.0 %all-gather.9.cloned.1.call-start = ((), (), s32[]{:S(2)}) async-start(), calls=%async_computation.6 | async-start | bytes 2506752 | tf_op jit(solution)/shard_map/all_gather | solution.py:118
  42.3 110.8 %copy-start.8 = (s32[2]{0:T(128)S(1)}, s32[2]{0:T(128)}, u32[]{:S(2)}) copy-start(s32[2]{0:T(128)} %param.19) | copy-start | bytes 28
  42.3 111.4 %copy-start.10 = (s32[2,128]{1,0:T(2,128)S(1)}, s32[2,128]{1,0:T(2,128)}, u32[]{:S(2)}) copy-start(s32[2,128]{1,0:T(2,128)} %param.23) | copy-start | bytes 3076
  42.4 111.7 %copy-start.11 = (s32[2]{0:T(128)S(1)}, s32[2]{0:T(128)}, u32[]{:S(2)}) copy-start(s32[2]{0:T(128)} %param.22) | copy-start | bytes 28
  42.4 112.4 %copy-start.6 = (bf16[128,64]{0,1:T(8,128)(2,1)S(1)}, bf16[128,64]{0,1:T(8,128)(2,1)}, u32[]{:S(2)}) copy-start(bf16[128,64]{0,1:T(8,128)(2,1)} %param.17) | copy-start | bytes 49156
  44.2 106.0 %all-to-all-start = ((bf16[32,64,192]{2,1,0:T(8,128)(2,1)}), bf16[32,64,192]{2,1,0:T(8,128)(2,1)S(1)}, u32[]{:S(2)}, u32[]{:S(2)}) async-start(bf16[32,64,192]{2,1,0:T(8,128)(2,1)} %stack.2), calls=%async_computation | async-start | bytes 2097152 | tf_op jit(solution)/shard_map/all_to_all | solution.py:108
  50.5 192.8 %all-gather.5.cloned.1.call-start = ((), (), s32[]{:S(2)}) async-start(), calls=%async_computation.3 | async-start | bytes 2506752 | tf_op jit(solution)/shard_map/all_gather | solution.py:134
  52.2 138.5 %copy-start.12 = (s32[2]{0:T(128)S(1)}, s32[2]{0:T(128)}, u32[]{:S(2)}) copy-start(s32[2]{0:T(128)} %param.20) | copy-start | bytes 28
  151.0 44.8 %copy-start.9 = (f32[512]{0:T(512)S(1)}, f32[512]{0:T(512)}, u32[]{:S(2)}) copy-start(f32[512]{0:T(512)} %param.15) | copy-start | bytes 6148
  152.3 182.5 %all-gather.7.cloned.1.call-start = ((), (), s32[]{:S(2)}) async-start(), calls=%async_computation.4 | async-start | bytes 2228224 | tf_op jit(solution)/shard_map/all_gather | solution.py:135
  153.1 393.3 %reduce-scatter.4.cloned.1.call-start = ((), (), s32[]{:S(2)}) async-start(), calls=%async_computation.5 | async-start | bytes 557056 | tf_op jit(solution)/shard_map/reduce_scatter | solution.py:180
  255.9 5.7 copy-start.1
  266.9 44.2 %copy-start.2 = (bf16[16,64,576]{2,1,0:T(8,128)(2,1)S(1)}, bf16[16,64,576]{2,1,0:T(8,128)(2,1)}, u32[]{:S(2)}) copy-start(bf16[16,64,576]{2,1,0:T(8,128)(2,1)} %param.18) | copy-start | bytes 3538948
  311.1 3.8 copy-start
  318.7 24.4 %copy-start.4 = (bf16[128,512]{0,1:T(8,128)(2,1)S(1)}, bf16[128,512]{0,1:T(8,128)(2,1)}, u32[]{:S(2)}) copy-start(bf16[128,512]{0,1:T(8,128)(2,1)} %multiply_convert_fusion) | copy-start | bytes 393220
  342.7 206.2 %copy-start.3 = (bf16[1024,576]{0,1:T(8,128)(2,1)S(1)}, bf16[1024,576]{0,1:T(8,128)(2,1)}, u32[]{:S(2)}) copy-start(bf16[1024,576]{0,1:T(8,128)(2,1)} %copy.98) | copy-start | bytes 3538948
  342.7 413.4 %reduce-scatter.6.cloned.1.call-start = ((), (), s32[]{:S(2)}) async-start(), calls=%async_computation.7 | async-start | bytes 557056 | tf_op jit(solution)/shard_map/reduce_scatter | solution.py:197
Sparse Core Ops, SparseCore 0:
  42.5 102.6 all-gather.8
  152.4 90.8 all-gather.4
  246.5 88.2 all-gather.6
  342.8 203.5 reduce-scatter.3
  551.3 204.7 reduce-scatter.5
